TPU v7x, 128 devices: a whole 4x4x4 slice. The times are simulated.
128 devices in a mesh: fsdp: 32 (over y, x_hi, z), red: 4 (over x_lo, core).
Axes of the slice: x: 4 (x_hi: 2, x_lo: 2; x = x_hi * 2 + x_lo), y: 4, z: 4, core: 2. Of those that a mesh axis runs over, the one named last changes fastest.
Arguments:
- layer_input: bfloat16 [2, 8192, 16384], P(None, 'fsdp', 'red'), may hold values from -6 to 6
- kv_cotangent: bfloat16 [2, 8192, 1024], P(None, 'fsdp'), may hold values from -16 to 16
- failed_member: int32 [32], P('fsdp'), may hold values from 0 to 4
- master: float32 [2, 1024, 16384], P(None, 'fsdp', 'red'), may hold values from -0.046875 to 0.046875
- first_moment: float32 [2, 1024, 16384], P(None, 'fsdp', 'red'), may hold values from -4 to 4
- second_moment: float32 [2, 1024, 16384], P(None, 'fsdp', 'red'), may hold values from 0.05 to 2
- loss_scale: float32 [32, 4], P('fsdp', 'red'), may hold values from 2 to 8
- spare_master: float32 [2, 1024, 16384], P(None, 'fsdp', 'red'), may hold values from -0.046875 to 0.046875
- spare_first: float32 [2, 1024, 16384], P(None, 'fsdp', 'red'), may hold values from -4 to 4
- spare_second: float32 [2, 1024, 16384], P(None, 'fsdp', 'red'), may hold values from 0.05 to 2
- spare_scale: float32 [32, 4], P('fsdp', 'red'), may hold values from 2 to 8
Outputs:
- kv_out: bfloat16 [2, 8192, 1024], P(None, 'fsdp', 'red')
- input_grad: bfloat16 [2, 8192, 16384], P(None, 'fsdp', 'red')
- new_master: float32 [2, 1024, 16384], P(None, 'fsdp', 'red')
- new_first: float32 [2, 1024, 16384], P(None, 'fsdp', 'red')
- new_second: float32 [2, 1024, 16384], P(None, 'fsdp', 'red')
Inputs may be any that keep to these rules, and one draw needn't show every extreme that they name: failed_member[f] is the member of redundancy group f (index along red) whose state was lost; the value 4 means that group lost nothing.
All inputs are finite; a program needn't handle non-finite values.
Results may differ from a plain program's by a relative error of at most 0.017.
Values may be sent and summed in bfloat16 or wider, within the bound.
A program may use at most 128 MiB of HBM per device.

v0:
```python
import functools
import jax
import jax.numpy as jnp
from jax import lax
from jax.sharding import Mesh
from jax.sharding import PartitionSpec as P

RED = ("red_0", "red_1")
FSDP = ("fsdp_0", "fsdp_1", "fsdp_2")
FSDP_RED = ("fsdp_0", "fsdp_1", "fsdp_2", "red_0", "red_1")
BETA_FIRST = 0.9
BETA_SECOND = 0.95
LEARN_RATE = 0.01
DECAY_RATE = 0.1
ADAM_EPS = 1e-08
MEAN_EPS = 1e-06


def shifted(shard, axis, by):
    length = lax.axis_size(axis)
    return lax.ppermute(shard, axis, [(i, (i + by) % length) for i in range(length)])


def cut_along(shard, dim, length):
    before, after = (shard.shape[:dim], shard.shape[dim + 1 :])
    return jnp.moveaxis(shard.reshape(*before, length, -1, *after), dim, 0)


def sent_and_summed(shard, axis, dim):
    length = lax.axis_size(axis)
    parts = lax.all_to_all(cut_along(shard, dim, length), axis, 0, 0, tiled=True)
    return jnp.sum(parts.astype(jnp.float32), axis=0)


def reduced_to_own(parts, axes, order):
    inside = parts.shape[1:]
    parts = parts.reshape(*(lax.axis_size(a) for a in axes), *inside)
    parts = jnp.moveaxis(parts, order, range(len(axes))).reshape(-1, *inside)
    for k in order:
        parts = lax.psum_scatter(parts, axes[k], scatter_dimension=0, tiled=True)
    return parts[0]


def summed_rows(shard, axes, order, dim):
    length = lax.axis_size(axes)
    return reduced_to_own(cut_along(shard, dim, length), axes, order)


def by_axis(shard, axes):
    return functools.reduce(lax.psum, axes, shard)


def local(
    layer_input,
    kv_cotangent,
    failed_member,
    master,
    first_moment,
    second_moment,
    loss_scale,
    spare_master,
    spare_first,
    spare_second,
    spare_scale,
):
    layers = master.shape[0]
    local_rows = master.shape[1]
    replaced = lax.axis_index(RED) == failed_member[0]
    copy_master, copy_first, copy_second, copy_scale = (
        shifted(spare_master.astype(jnp.bfloat16), RED, 1).astype(spare_master.dtype),
        shifted(spare_first.astype(jnp.bfloat16), RED, 1).astype(spare_first.dtype),
        shifted(spare_second.astype(jnp.bfloat16), RED, 1).astype(spare_second.dtype),
        shifted(spare_scale.astype(jnp.bfloat16), RED, 1).astype(spare_scale.dtype),
    )
    master_now = jnp.where(replaced, copy_master, master)
    first_now = jnp.where(replaced, copy_first, first_moment)
    second_now = jnp.where(replaced, copy_second, second_moment)
    scale_now = jnp.where(replaced, copy_scale, loss_scale)
    weights = master_now.astype(jnp.bfloat16)
    gathered = lax.all_gather(weights, FSDP, axis=1, tiled=True)
    kv_list = []
    input_list = []
    for layer_index in range(layers):
        inputs = layer_input[layer_index]
        upstream = kv_cotangent[layer_index]
        full_weight = gathered[layer_index]
        partial_kv = lax.dot_general(
            inputs, full_weight, (((1,), (1,)), ((), ())), preferred_element_type=jnp.float32
        )
        kv_list.append(
            sent_and_summed(partial_kv.astype(jnp.bfloat16), RED, 1).astype(jnp.bfloat16)
        )
        input_list.append(
            jnp.dot(upstream, full_weight, preferred_element_type=jnp.float32).astype(jnp.bfloat16)
        )
    grad_terms = jnp.einsum(
        "ltc,ltd->lcd", kv_cotangent, layer_input, preferred_element_type=jnp.float32
    )
    grad_sum = summed_rows(grad_terms.astype(jnp.bfloat16), FSDP, (0, 2, 1), 1).astype(jnp.float32)
    gradient = grad_sum / scale_now[0, 0]
    total_squares = by_axis(jnp.sum(gradient * gradient), FSDP_RED)
    entries = layers * local_rows * lax.axis_size(FSDP) * master.shape[2] * lax.axis_size(RED)
    factor = jnp.minimum(1.0, lax.rsqrt(total_squares / entries + MEAN_EPS))
    clipped = gradient * factor
    new_first = BETA_FIRST * first_now + (1.0 - BETA_FIRST) * clipped
    new_second = BETA_SECOND * second_now + (1.0 - BETA_SECOND) * clipped * clipped
    new_master = master_now - LEARN_RATE * (
        new_first / (jnp.sqrt(new_second) + ADAM_EPS) + DECAY_RATE * master_now
    )
    return (jnp.stack(kv_list), jnp.stack(input_list), new_master, new_first, new_second)


def solution(mesh):
    split = Mesh(
        mesh.devices.reshape(4, 2, 4, 2, 2), ("fsdp_0", "fsdp_1", "fsdp_2", "red_0", "red_1")
    )
    placed = (
        P(None, FSDP, RED),
        P(None, FSDP, None),
        P(FSDP),
        P(None, FSDP, RED),
        P(None, FSDP, RED),
        P(None, FSDP, RED),
        P(FSDP, RED),
        P(None, FSDP, RED),
        P(None, FSDP, RED),
        P(None, FSDP, RED),
        P(FSDP, RED),
    )
    return jax.shard_map(
        local,
        mesh=split,
        in_specs=placed,
        out_specs=(
            P(None, FSDP, RED),
            P(None, FSDP, RED),
            P(None, FSDP, RED),
            P(None, FSDP, RED),
            P(None, FSDP, RED),
        ),
        check_vma=False,
    )
```

profile of v0, /device:TPU:1, one launch (start us, length us, event | category | flops | bytes accessed | tf_op | source)
XLA Modules:
  0.0 369.4 jit_solution(7072015989123471790)
XLA Ops:
  8.0 12.8 %convolution_convert_fusion = bf16[2,1024,4096]{2,1,0:T(8,128)(2,1)} fusion(bf16[2,256,1024]{2,1,0:T(8,128)(2,1)} %param.12, bf16[2,256,4096]{2,1,0:T(8,128)(2,1)} %param.11), kind=kOutput, calls=%fused_computation | convolution fusion | flops 4303355904 | bytes 22020096 | tf_op jit(solution)/shard_map/ltc,ltd->lcd/dot_general | solution.py:96
  20.8 14.0 %copy.20 = bf16[4,2,4,2,32,4096]{5,4,3,1,2,0:T(8,128)(2,1)} copy(bf16[4,2,4,2,32,4096]{5,4,2,1,0,3:T(8,128)(2,1)} %bitcast.78) | data formatting | bytes 33554432 | tf_op jit(solution)/shard_map/reshape | solution.py:37
  36.1 2.7 collective-permute-start
  39.4 5.5 %collective-permute-done = bf16[2,32,4096]{2,1,0:T(8,128)(2,1)S(1)} collective-permute-done((bf16[2,32,4096]{2,1,0:T(8,128)(2,1)S(1)}, bf16[2,32,4096]{2,1,0:T(8,128)(2,1)S(1)}, u32[]{:S(2)}, u32[]{:S(2)}) %collective-permute-start) | collective-permute-done | bytes 524320 | tf_op jit(solution)/shard_map/ppermute | solution.py:21
  45.9 179.6 %reduce-scatter.4.cloned.1.call-done = bf16[8,2,32,4096]{3,2,1,0:T(8,128)(2,1)} async-done(((bf16[32,2,32,4096]{3,2,1,0:T(8,128)(2,1)}), bf16[8,2,32,4096]{3,2,1,0:T(8,128)(2,1)}) %reduce-scatter.4.cloned.1.call-update) | async-done | bytes 4194320 | tf_op jit(solution)/shard_map/reduce_scatter | solution.py:40
  226.2 2.9 collective-permute-start.2
  229.1 2.1 convert_element_type.73
  234.0 13.6 %all-gather.2.cloned.1.call-done = bf16[2,1024,4096]{2,1,0:T(8,128)(2,1)} async-done(((bf16[2,32,4096]{2,1,0:T(8,128)(2,1)}), bf16[2,1024,4096]{2,1,0:T(8,128)(2,1)}) %all-gather.2.cloned.1.call-update) | async-done | bytes 16777232 | tf_op jit(solution)/shard_map/all_gather | solution.py:80
  247.6 7.3 %fusion.12 = bf16[1024,256]{1,0:T(8,128)(2,1)} fusion(bf16[2,256,4096]{2,1,0:T(8,128)(2,1)} %param.11, bf16[2,1024,4096]{2,1,0:T(8,128)(2,1)} %all-gather.2.cloned.1.call-done), kind=kOutput, calls=%fused_computation.17 | convolution fusion | flops 2147745792 | bytes 11010048 | tf_op jit(solution)/shard_map/dot_general | solution.py:87
  254.9 4.9 %all-to-all-start.1 = ((bf16[4,256,256]{1,2,0:T(8,128)(2,1)}), bf16[4,256,256]{1,2,0:T(8,128)(2,1)S(1)}, u32[]{:S(2)}, u32[]{:S(2)}) async-start(bf16[4,256,256]{1,2,0:T(8,128)(2,1)} %bitcast.11), calls=%async_computation.1 | async-start | bytes 1048576 | tf_op jit(solution)/shard_map/all_to_all | solution.py:31
  259.7 7.3 %fusion.15 = bf16[1024,256]{1,0:T(8,128)(2,1)} fusion(bf16[2,256,4096]{2,1,0:T(8,128)(2,1)} %param.11, bf16[2,1024,4096]{2,1,0:T(8,128)(2,1)} %all-gather.2.cloned.1.call-done), kind=kOutput, calls=%fused_computation.18 | convolution fusion | flops 2147745792 | bytes 11010048 | tf_op jit(solution)/shard_map/dot_general | solution.py:87
  267.1 12.1 %reduce-scatter.6.cloned.1.call-done = bf16[2,2,32,4096]{3,2,1,0:T(8,128)(2,1)} async-done(((bf16[8,2,32,4096]{3,2,1,0:T(8,128)(2,1)}), bf16[2,2,32,4096]{3,2,1,0:T(8,128)(2,1)}) %reduce-scatter.6.cloned.1.call-update) | async-done | bytes 1048592 | tf_op jit(solution)/shard_map/reduce_scatter | solution.py:40
  279.2 7.2 %fusion.6 = bf16[1,256,4096]{1,2,0:T(8,128)(2,1)} fusion(bf16[2,1024,4096]{2,1,0:T(8,128)(2,1)} %all-gather.2.cloned.1.call-done, bf16[2,256,1024]{2,1,0:T(8,128)(2,1)S(1)} %copy-done.4), kind=kOutput, calls=%fused_computation.9 | convolution fusion | flops 2148532224 | bytes 11010048 | tf_op jit(solution)/shard_map/dot_general | solution.py:94
  286.4 7.2 %fusion.7 = bf16[1,256,4096]{1,2,0:T(8,128)(2,1)} fusion(bf16[2,1024,4096]{2,1,0:T(8,128)(2,1)} %all-gather.2.cloned.1.call-done, bf16[2,256,1024]{2,1,0:T(8,128)(2,1)S(1)} %copy-done.4), kind=kOutput, calls=%fused_computation.10 | convolution fusion | flops 2148532224 | bytes 11010048 | tf_op jit(solution)/shard_map/dot_general | solution.py:94
  293.6 5.0 %all-to-all-start = ((bf16[4,256,256]{1,2,0:T(8,128)(2,1)}), bf16[4,256,256]{1,2,0:T(8,128)(2,1)S(1)}, u32[]{:S(2)}, u32[]{:S(2)}) async-start(bf16[4,256,256]{1,2,0:T(8,128)(2,1)} %bitcast.79), calls=%async_computation | async-start | bytes 1048576 | tf_op jit(solution)/shard_map/all_to_all | solution.py:31
  298.7 4.6 %pad_maximum_fusion = bf16[2,256,4096]{1,2,0:T(8,128)(2,1)} fusion(bf16[1,256,4096]{1,2,0:T(8,128)(2,1)} %fusion.7, bf16[1,256,4096]{1,2,0:T(8,128)(2,1)} %fusion.6), kind=kLoop, calls=%fused_computation.11 | loop fusion | flops 2097152 | bytes 8388608 | tf_op jit(solution)/shard_map/stack | solution.py:110
  303.2 4.0 %reduce-scatter.8.cloned.1.call-done = bf16[1,2,32,4096]{3,2,1,0:T(8,128)(2,1)} async-done(((bf16[2,2,32,4096]{3,2,1,0:T(8,128)(2,1)}), bf16[1,2,32,4096]{3,2,1,0:T(8,128)(2,1)}) %reduce-scatter.8.cloned.1.call-update) | async-done | bytes 524304 | tf_op jit(solution)/shard_map/reduce_scatter | solution.py:40
  309.1 6.4 %copy.22 = bf16[2,256,4096]{2,1,0:T(8,128)(2,1)} copy(bf16[2,256,4096]{1,2,0:T(8,128)(2,1)} %pad_maximum_fusion) | data formatting | bytes 8388608
  315.5 9.1 %psum.35 = f32[]{:T(128)} all-reduce(f32[]{:T(128)} %multiply_reduce_fusion), channel_id=1, replica_groups=mesh['fsdp_0'=4,'fsdp_1'=2,'fsdp_2'=4,'red_0'=2,'red_1'=2] {'fsdp_0'}, use_global_device_ids=true, to_apply=%region_6.7 | all-reduce | flops 1 | bytes 8 | tf_op jit(solution)/shard_map/psum | solution.py:50
  324.6 5.9 %psum.36 = f32[]{:T(128)} all-reduce(f32[]{:T(128)} %psum.35), channel_id=1, replica_groups=mesh['fsdp_0'=4,'fsdp_1'=2,'fsdp_2'=4,'red_0'=2,'red_1'=2] {'fsdp_1'}, use_global_device_ids=true, to_apply=%region_7.8 | all-reduce | flops 1 | bytes 8 | tf_op jit(solution)/shard_map/psum | solution.py:50
  330.6 11.5 %psum.37 = f32[]{:T(128)} all-reduce(f32[]{:T(128)} %psum.36), channel_id=1, replica_groups=mesh['fsdp_0'=4,'fsdp_1'=2,'fsdp_2'=4,'red_0'=2,'red_1'=2] {'fsdp_2'}, use_global_device_ids=true, to_apply=%region_8.9 | all-reduce | flops 1 | bytes 8 | tf_op jit(solution)/shard_map/psum | solution.py:50
  342.2 4.4 %psum.38 = f32[]{:T(128)} all-reduce(f32[]{:T(128)} %psum.37), channel_id=1, replica_groups=mesh['fsdp_0'=4,'fsdp_1'=2,'fsdp_2'=4,'red_0'=2,'red_1'=2] {'red_0'}, use_global_device_ids=true, to_apply=%region_9.10 | all-reduce | flops 1 | bytes 8 | tf_op jit(solution)/shard_map/psum | solution.py:50
  347.4 10.6 %psum.39 = f32[]{:T(128)} all-reduce(f32[]{:T(128)} %psum.38), channel_id=1, replica_groups=mesh['fsdp_0'=4,'fsdp_1'=2,'fsdp_2'=4,'red_0'=2,'red_1'=2] {'red_1'}, use_global_device_ids=true, to_apply=%region_10.11 | all-reduce | flops 1 | bytes 8 | tf_op jit(solution)/shard_map/psum | solution.py:50
  358.7 3.5 multiply_subtract_fusion
  (33 shorter events, 6.8 us)
Async XLA Ops:
  8.0 217.5 %reduce-scatter.4.cloned.1.call-start = ((), (), s32[]{:S(2)}) async-start(), calls=%async_computation.6 | async-start | bytes 20971520 | tf_op jit(solution)/shard_map/reduce_scatter | solution.py:40
  34.8 1.2 copy-start.2
  34.8 10.1 %copy-start = (f32[2,32,4096]{2,1,0:T(8,128)S(1)}, f32[2,32,4096]{2,1,0:T(8,128)}, u32[]{:S(2)}) copy-start(f32[2,32,4096]{2,1,0:T(8,128)} %param.14) | copy-start | bytes 3145732
  34.9 212.7 %all-gather.2.cloned.1.call-start = ((), (), s32[]{:S(2)}) async-start(), calls=%async_computation.5 | async-start | bytes 17301504 | tf_op jit(solution)/shard_map/all_gather | solution.py:80
  36.1 8.8 %collective-permute-start = (bf16[2,32,4096]{2,1,0:T(8,128)(2,1)S(1)}, bf16[2,32,4096]{2,1,0:T(8,128)(2,1)S(1)}, u32[]{:S(2)}, u32[]{:S(2)}) collective-permute-start(bf16[2,32,4096]{2,1,0:T(8,128)(2,1)S(1)} %convert_element_type.62), channel_id=1, source_target_pairs={{0,1},{1,2},{2,3},{3,0},{4,5},{5,6},{6,7},{7,4},{8,9},{9,10},{10,1... | collective-permute-start | bytes 1572872 | tf_op jit(solution)/shard_map/ppermute | solution.py:21
  39.4 191.9 %copy-start.3 = (f32[2,32,4096]{2,1,0:T(8,128)S(1)}, f32[2,32,4096]{2,1,0:T(8,128)}, u32[]{:S(2)}) copy-start(f32[2,32,4096]{2,1,0:T(8,128)} %param.20) | copy-start | bytes 3145732
  45.8 233.3 %reduce-scatter.6.cloned.1.call-start = ((), (), s32[]{:S(2)}) async-start(), calls=%async_computation.7 | async-start | bytes 5242880 | tf_op jit(solution)/shard_map/reduce_scatter | solution.py:40
  226.2 7.2 %collective-permute-start.2 = (bf16[1,1]{1,0:T(2,128)(2,1)}, bf16[1,1]{1,0:T(2,128)(2,1)}, u32[]{:S(2)}, u32[]{:S(2)}) collective-permute-start(bf16[1,1]{1,0:T(2,128)(2,1)} %convert_element_type.77), channel_id=1, source_target_pairs={{0,1},{1,2},{2,3},{3,0},{4,5},{5,6},{6,7},{7,4},{8,9},{9,10},{10,1... | collective-permute-start | bytes 14 | tf_op jit(solution)/shard_map/ppermute | solution.py:21
  231.2 127.5 %collective-permute-start.1 = (bf16[2,32,4096]{2,1,0:T(8,128)(2,1)}, bf16[2,32,4096]{2,1,0:T(8,128)(2,1)}, u32[]{:S(2)}, u32[]{:S(2)}) collective-permute-start(bf16[2,32,4096]{2,1,0:T(8,128)(2,1)} %convert_element_type.73), channel_id=1, source_target_pairs={{0,1},{1,2},{2,3},{3,0},{4,5},{5,6},{6,7},{7,4},{8,9},{9,10},{10,1... | collective-permute-start | bytes 1572872 | tf_op jit(solution)/shard_map/ppermute | solution.py:21
  232.1 126.6 %collective-permute-start.3 = (bf16[2,32,4096]{2,1,0:T(8,128)(2,1)}, bf16[2,32,4096]{2,1,0:T(8,128)(2,1)}, u32[]{:S(2)}, u32[]{:S(2)}) collective-permute-start(bf16[2,32,4096]{2,1,0:T(8,128)(2,1)} %convert_element_type.79), channel_id=1, source_target_pairs={{0,1},{1,2},{2,3},{3,0},{4,5},{5,6},{6,7},{7,4},{8,9},{9,10},{10,1... | collective-permute-start | bytes 1572872 | tf_op jit(solution)/shard_map/ppermute | solution.py:21
  254.9 38.8 %all-to-all-start.1 = ((bf16[4,256,256]{1,2,0:T(8,128)(2,1)}), bf16[4,256,256]{1,2,0:T(8,128)(2,1)S(1)}, u32[]{:S(2)}, u32[]{:S(2)}) async-start(bf16[4,256,256]{1,2,0:T(8,128)(2,1)} %bitcast.11), calls=%async_computation.1 | async-start | bytes 1048576 | tf_op jit(solution)/shard_map/all_to_all | solution.py:31
  259.7 19.4 %copy-start.4 = (bf16[2,256,1024]{2,1,0:T(8,128)(2,1)S(1)}, bf16[2,256,1024]{2,1,0:T(8,128)(2,1)}, u32[]{:S(2)}) copy-start(bf16[2,256,1024]{2,1,0:T(8,128)(2,1)} %param.12) | copy-start | bytes 3145732
  259.7 47.5 %reduce-scatter.8.cloned.1.call-start = ((), (), s32[]{:S(2)}) async-start(), calls=%async_computation.8 | async-start | bytes 1572864 | tf_op jit(solution)/shard_map/reduce_scatter | solution.py:40
  293.6 36.9 %all-to-all-start = ((bf16[4,256,256]{1,2,0:T(8,128)(2,1)}), bf16[4,256,256]{1,2,0:T(8,128)(2,1)S(1)}, u32[]{:S(2)}, u32[]{:S(2)}) async-start(bf16[4,256,256]{1,2,0:T(8,128)(2,1)} %bitcast.79), calls=%async_computation | async-start | bytes 1048576 | tf_op jit(solution)/shard_map/all_to_all | solution.py:31
  309.1 49.6 %copy-start.1 = (bf16[1,2,32,4096]{3,2,1,0:T(8,128)(2,1)S(1)}, bf16[1,2,32,4096]{3,2,1,0:T(8,128)(2,1)}, u32[]{:S(2)}) copy-start(bf16[1,2,32,4096]{3,2,1,0:T(8,128)(2,1)} %reduce-scatter.8.cloned.1.call-done) | copy-start | bytes 1572868
Sparse Core Ops, SparseCore 0:
  35.0 190.4 reduce-scatter.3
  227.9 51.1 reduce-scatter.5
  281.5 25.6 reduce-scatter.7
Sparse Core Ops, SparseCore 1:
  45.9 201.7 all-gather.1
where the time goes:
time: 370 us; the launch traced here: 369 us
  waiting for transfers between devices  215 us (58%)
  matrix products  41.8 us (11%)
  blocking collectives  41.5 us (11%)
  local copies, waits for them, and re-layouts  22.4 us (6%)
  between operations  18.5 us (5%)
  starting transfers between devices  16.3 us (4%)
  other arithmetic  14.1 us (4%)
    reduce_scatter x3, waiting for transfers between devices, reduced_to_own(): parts = lax.psum_scatter(parts, axes[k], scatter_dimension=0, tiled=True)  196 us
    psum x5, blocking collectives, by_axis(): return functools.reduce(lax.psum, axes, shard)  41.5 us
    dot_general x2, matrix products, local(): lax.dot_general(inputs, full_weight, (((1,), (1,)), ((), ())), preferred_...  14.6 us
    dot_general x2, matrix products, local(): jnp.dot(upstream, full_weight, preferred_element_type=jnp.float32)  14.5 us
    reshape x1, local copies, waits for them, and re-layouts, reduced_to_own(): parts = parts.reshape(*(lax.axis_size(a) for a in axes), *inside)  14 us
    all_gather x1, waiting for transfers between devices, local(): gathered = lax.all_gather(weights, FSDP, axis=1, tiled=True)  13.6 us
    dot_general x1, matrix products, local(): jnp.einsum('ltc,ltd->lcd', kv_cotangent, layer_input, preferred_element_t...  12.8 us
    all_to_all x2, starting transfers between devices, sent_and_summed(): lax.all_to_all(cut_along(shard, dim, length), axis, 0, 0, tiled=True)  9.91 us
  transfers between devices with their start and end apart: 10, of which 5 were waited for; matrix products, arithmetic and copies ran while one was open for 13% of the time, Pallas kernels for 0%

commit v1 on v0

--- a/solution.py
+++ b/solution.py
@@ -77,7 +77,12 @@
     second_now = jnp.where(replaced, copy_second, second_moment)
     scale_now = jnp.where(replaced, copy_scale, loss_scale)
     weights = master_now.astype(jnp.bfloat16)
-    gathered = lax.all_gather(weights, FSDP, axis=1, tiled=True)
+    gathered = jnp.concatenate(
+        lax.all_to_all(
+            jnp.stack([weights] * lax.axis_size(FSDP), 0), FSDP, split_axis=0, concat_axis=0
+        ),
+        1,
+    )
     kv_list = []
     input_list = []
     for layer_index in range(layers):

time: 370 us -> 546 us (1.48)
  waiting for transfers between devices: 215 us -> 372 us
  local copies, waits for them, and re-layouts: 22.4 us -> 41.6 us
  starting transfers between devices: 16.3 us -> 27 us
  blocking collectives: 41.5 us -> 35.7 us
    reduce_scatter x3, waiting for transfers between devices: 196 us -> 367 us  [reduced_to_own(): parts = lax.psum_scatter(parts, axes[k], scatter_dimension=0, tiled=True)]
    all_gather x1 -> x0, waiting for transfers between devices: 13.6 us -> none  [local(): gathered = lax.all_gather(weights, FSDP, axis=1, tiled=True)]
    all_to_all x0 -> x1, starting transfers between devices: none -> 10.4 us  [local(): lax.all_to_all(jnp.stack([weights] * lax.axis_size(FSDP), 0), FSDP, split...]
    slice x0 -> x1, local copies, waits for them, and re-layouts: none -> 9.62 us  [local(): full_weight = gathered[layer_index]]
    another operation x0 -> x1, local copies, waits for them, and re-layouts: none -> 6.26 us  [local(): jnp.stack([weights] * lax.axis_size(FSDP), 0)]
    psum x5, blocking collectives: 41.5 us -> 35.7 us  [by_axis(): return functools.reduce(lax.psum, axes, shard)]
    unnamed x12 -> x18, local copies, waits for them, and re-layouts: 8.38 us -> 11.7 us
  transfers between devices with their start and end apart: 10 -> 10, of which waited for: 5 -> 3; matrix products, arithmetic and copies ran while one was open for 13% -> 11% of each run, Pallas kernels for 0% -> 0%
where the time goes in v1:
time: 546 us; the launch traced here: 545 us
  waiting for transfers between devices  372 us (68%)
  local copies, waits for them, and re-layouts  41.6 us (8%)
  matrix products  37.6 us (7%)
  blocking collectives  35.7 us (7%)
  starting transfers between devices  27 us (5%)
  between operations  17.1 us (3%)
  other arithmetic  13.3 us (2%)
    reduce_scatter x3, waiting for transfers between devices, reduced_to_own(): parts = lax.psum_scatter(parts, axes[k], scatter_dimension=0, tiled=True)  367 us
    psum x5, blocking collectives, by_axis(): return functools.reduce(lax.psum, axes, shard)  35.7 us
    dot_general x2, matrix products, local(): jnp.dot(upstream, full_weight, preferred_element_type=jnp.float32)  14.5 us
    reshape x1, local copies, waits for them, and re-layouts, reduced_to_own(): parts = parts.reshape(*(lax.axis_size(a) for a in axes), *inside)  14 us
    dot_general x1, matrix products, local(): jnp.einsum('ltc,ltd->lcd', kv_cotangent, layer_input, preferred_element_t...  12.8 us
    unnamed x18, local copies, waits for them, and re-layouts  11.7 us
  transfers between devices with their start and end apart: 10, of which 3 were waited for; matrix products, arithmetic and copies ran while one was open for 11% of the time, Pallas kernels for 0%

profile of v1, /device:TPU:1, one launch (start us, length us, event | category | flops | bytes accessed | tf_op | source)
XLA Modules:
  0.0 544.6 jit_solution(18169683267736046456)
XLA Ops:
  7.2 12.8 %convolution_convert_fusion = bf16[2,1024,4096]{2,1,0:T(8,128)(2,1)} fusion(bf16[2,256,1024]{2,1,0:T(8,128)(2,1)} %param.12, bf16[2,256,4096]{2,1,0:T(8,128)(2,1)} %param.11), kind=kOutput, calls=%fused_computation | convolution fusion | flops 4303355904 | bytes 22020096 | tf_op jit(solution)/shard_map/ltc,ltd->lcd/dot_general | solution.py:101
  20.0 14.0 %copy.20 = bf16[4,2,4,2,32,4096]{5,4,3,1,2,0:T(8,128)(2,1)} copy(bf16[4,2,4,2,32,4096]{5,4,2,1,0,3:T(8,128)(2,1)} %bitcast.65) | data formatting | bytes 33554432 | tf_op jit(solution)/shard_map/reshape | solution.py:37
  38.6 5.5 %collective-permute-done = bf16[2,32,4096]{2,1,0:T(8,128)(2,1)S(1)} collective-permute-done((bf16[2,32,4096]{2,1,0:T(8,128)(2,1)S(1)}, bf16[2,32,4096]{2,1,0:T(8,128)(2,1)S(1)}, u32[]{:S(2)}, u32[]{:S(2)}) %collective-permute-start) | collective-permute-done | bytes 524320 | tf_op jit(solution)/shard_map/ppermute | solution.py:21
  44.2 6.3 %stack.14 = bf16[32,2,32,4096]{3,2,1,0:T(8,128)(2,1)} broadcast(bf16[2,32,4096]{2,1,0:T(8,128)(2,1)S(1)} %fusion.16), dimensions={1,2,3} | broadcast | bytes 17301504 | tf_op jit(solution)/shard_map/stack | solution.py:82
  50.4 10.4 %all-to-all-start = ((bf16[32,2,32,4096]{3,2,1,0:T(8,128)(2,1)}), bf16[32,2,32,4096]{3,2,1,0:T(8,128)(2,1)}, u32[]{:S(2)}, u32[]{:S(2)}) async-start(bf16[32,2,32,4096]{3,2,1,0:T(8,128)(2,1)} %stack.14), calls=%async_computation | async-start | bytes 33554432 | tf_op jit(solution)/shard_map/all_to_all | solution.py:81
  60.9 327.1 %reduce-scatter.4.cloned.1.call-done = bf16[8,2,32,4096]{3,2,1,0:T(8,128)(2,1)} async-done(((bf16[32,2,32,4096]{3,2,1,0:T(8,128)(2,1)}), bf16[8,2,32,4096]{3,2,1,0:T(8,128)(2,1)}) %reduce-scatter.4.cloned.1.call-update) | async-done | bytes 4194320 | tf_op jit(solution)/shard_map/reduce_scatter | solution.py:40
  388.7 5.7 %collective-permute-start.2 = (bf16[1,1]{1,0:T(2,128)(2,1)}, bf16[1,1]{1,0:T(2,128)(2,1)}, u32[]{:S(2)}, u32[]{:S(2)}) collective-permute-start(bf16[1,1]{1,0:T(2,128)(2,1)} %convert_element_type.77), channel_id=1, source_target_pairs={{0,1},{1,2},{2,3},{3,0},{4,5},{5,6},{6,7},{7,4},{8,9},{9,10},{10,1... | collective-permute-start | bytes 14 | tf_op jit(solution)/shard_map/ppermute | solution.py:21
  398.8 9.6 %fusion.23 = (bf16[1,32,32,4096]{3,2,0,1:T(8,128)(2,1)}, bf16[1,32,32,4096]{3,2,0,1:T(8,128)(2,1)S(1)}) fusion(bf16[2,32,32,4096]{3,2,0,1:T(8,128)(2,1)} %bitcast.1), kind=kLoop, calls=%fused_computation.28 | loop fusion | bytes 33554432 | tf_op jit(solution)/shard_map/slice | solution.py:91
  408.4 3.2 copy-done
  411.7 3.2 fusion.11
  414.8 39.6 %reduce-scatter.6.cloned.1.call-done = bf16[2,2,32,4096]{3,2,1,0:T(8,128)(2,1)} async-done(((bf16[8,2,32,4096]{3,2,1,0:T(8,128)(2,1)}), bf16[2,2,32,4096]{3,2,1,0:T(8,128)(2,1)}) %reduce-scatter.6.cloned.1.call-update) | async-done | bytes 1048592 | tf_op jit(solution)/shard_map/reduce_scatter | solution.py:40
  454.5 7.3 %fusion = bf16[1,256,4096]{1,2,0:T(8,128)(2,1)} fusion(bf16[1024,4096]{1,0:T(8,128)(2,1)} %bitcast.68, bf16[2,256,1024]{2,1,0:T(8,128)(2,1)S(1)} %copy-done.6), kind=kOutput, calls=%fused_computation.3 | convolution fusion | flops 2148532224 | bytes 11010048 | tf_op jit(solution)/shard_map/dot_general | solution.py:99
  461.8 4.2 all-to-all-start.2
  466.0 7.2 %fusion.8 = bf16[1024,256]{1,0:T(8,128)(2,1)} fusion(bf16[1024,4096]{1,0:T(8,128)(2,1)} %bitcast.69, bf16[2,256,4096]{2,1,0:T(8,128)(2,1)} %param.11), kind=kOutput, calls=%fused_computation.13 | convolution fusion | flops 2147745792 | bytes 11010048 | tf_op jit(solution)/shard_map/dot_general | solution.py:92
  473.2 7.2 %fusion.1 = bf16[1,256,4096]{1,2,0:T(8,128)(2,1)} fusion(bf16[1024,4096]{1,0:T(8,128)(2,1)} %bitcast.67, bf16[2,256,1024]{2,1,0:T(8,128)(2,1)S(1)} %copy-done.7), kind=kOutput, calls=%fused_computation.4 | convolution fusion | flops 2148532224 | bytes 11010048 | tf_op jit(solution)/shard_map/dot_general | solution.py:99
  480.4 3.8 all-to-all-start.1
  484.2 4.5 pad_maximum_fusion
  490.7 6.4 %copy.22 = bf16[2,256,4096]{2,1,0:T(8,128)(2,1)} copy(bf16[2,256,4096]{1,2,0:T(8,128)(2,1)} %pad_maximum_fusion) | data formatting | bytes 8388608
  497.0 9.1 %psum.35 = f32[]{:T(128)} all-reduce(f32[]{:T(128)} %multiply_reduce_fusion), channel_id=1, replica_groups=mesh['fsdp_0'=4,'fsdp_1'=2,'fsdp_2'=4,'red_0'=2,'red_1'=2] {'fsdp_0'}, use_global_device_ids=true, to_apply=%region_6.7 | all-reduce | flops 1 | bytes 8 | tf_op jit(solution)/shard_map/psum | solution.py:50
  506.2 5.9 %psum.36 = f32[]{:T(128)} all-reduce(f32[]{:T(128)} %psum.35), channel_id=1, replica_groups=mesh['fsdp_0'=4,'fsdp_1'=2,'fsdp_2'=4,'red_0'=2,'red_1'=2] {'fsdp_1'}, use_global_device_ids=true, to_apply=%region_7.8 | all-reduce | flops 1 | bytes 8 | tf_op jit(solution)/shard_map/psum | solution.py:50
  512.2 7.2 %psum.37 = f32[]{:T(128)} all-reduce(f32[]{:T(128)} %psum.36), channel_id=1, replica_groups=mesh['fsdp_0'=4,'fsdp_1'=2,'fsdp_2'=4,'red_0'=2,'red_1'=2] {'fsdp_2'}, use_global_device_ids=true, to_apply=%region_8.9 | all-reduce | flops 1 | bytes 8 | tf_op jit(solution)/shard_map/psum | solution.py:50
  519.4 4.7 psum.38
  525.0 8.8 %psum.39 = f32[]{:T(128)} all-reduce(f32[]{:T(128)} %psum.38), channel_id=1, replica_groups=mesh['fsdp_0'=4,'fsdp_1'=2,'fsdp_2'=4,'red_0'=2,'red_1'=2] {'red_1'}, use_global_device_ids=true, to_apply=%region_10.11 | all-reduce | flops 1 | bytes 8 | tf_op jit(solution)/shard_map/psum | solution.py:50
  534.5 3.5 multiply_subtract_fusion
  (40 shorter events, 10.2 us)
Async XLA Ops:
  7.2 380.8 %reduce-scatter.4.cloned.1.call-start = ((), (), s32[]{:S(2)}) async-start(), calls=%async_computation.6 | async-start | bytes 20971520 | tf_op jit(solution)/shard_map/reduce_scatter | solution.py:40
  34.0 1.2 copy-start.4
  34.0 10.1 %copy-start.1 = (f32[2,32,4096]{2,1,0:T(8,128)S(1)}, f32[2,32,4096]{2,1,0:T(8,128)}, u32[]{:S(2)}) copy-start(f32[2,32,4096]{2,1,0:T(8,128)} %param.14) | copy-start | bytes 3145732
  35.3 8.8 %collective-permute-start = (bf16[2,32,4096]{2,1,0:T(8,128)(2,1)S(1)}, bf16[2,32,4096]{2,1,0:T(8,128)(2,1)S(1)}, u32[]{:S(2)}, u32[]{:S(2)}) collective-permute-start(bf16[2,32,4096]{2,1,0:T(8,128)(2,1)S(1)} %convert_element_type.62), channel_id=1, source_target_pairs={{0,1},{1,2},{2,3},{3,0},{4,5},{5,6},{6,7},{7,4},{8,9},{9,10},{10,1... | collective-permute-start | bytes 1572872 | tf_op jit(solution)/shard_map/ppermute | solution.py:21
  50.4 348.4 %all-to-all-start = ((bf16[32,2,32,4096]{3,2,1,0:T(8,128)(2,1)}), bf16[32,2,32,4096]{3,2,1,0:T(8,128)(2,1)}, u32[]{:S(2)}, u32[]{:S(2)}) async-start(bf16[32,2,32,4096]{3,2,1,0:T(8,128)(2,1)} %stack.14), calls=%async_computation | async-start | bytes 33554432 | tf_op jit(solution)/shard_map/all_to_all | solution.py:81
  60.8 333.6 %copy-start.5 = (f32[2,32,4096]{2,1,0:T(8,128)S(1)}, f32[2,32,4096]{2,1,0:T(8,128)}, u32[]{:S(2)}) copy-start(f32[2,32,4096]{2,1,0:T(8,128)} %param.19) | copy-start | bytes 3145732
  60.8 393.6 %reduce-scatter.6.cloned.1.call-start = ((), (), s32[]{:S(2)}) async-start(), calls=%async_computation.7 | async-start | bytes 5242880 | tf_op jit(solution)/shard_map/reduce_scatter | solution.py:40
  388.0 100.7 %reduce-scatter.8.cloned.1.call-start = ((), (), s32[]{:S(2)}) async-start(), calls=%async_computation.8 | async-start | bytes 1572864 | tf_op jit(solution)/shard_map/reduce_scatter | solution.py:40
  388.7 9.4 %collective-permute-start.2 = (bf16[1,1]{1,0:T(2,128)(2,1)}, bf16[1,1]{1,0:T(2,128)(2,1)}, u32[]{:S(2)}, u32[]{:S(2)}) collective-permute-start(bf16[1,1]{1,0:T(2,128)(2,1)} %convert_element_type.77), channel_id=1, source_target_pairs={{0,1},{1,2},{2,3},{3,0},{4,5},{5,6},{6,7},{7,4},{8,9},{9,10},{10,1... | collective-permute-start | bytes 14 | tf_op jit(solution)/shard_map/ppermute | solution.py:21
  395.3 139.2 %collective-permute-start.1 = (bf16[2,32,4096]{2,1,0:T(8,128)(2,1)}, bf16[2,32,4096]{2,1,0:T(8,128)(2,1)}, u32[]{:S(2)}, u32[]{:S(2)}) collective-permute-start(bf16[2,32,4096]{2,1,0:T(8,128)(2,1)} %convert_element_type.73), channel_id=1, source_target_pairs={{0,1},{1,2},{2,3},{3,0},{4,5},{5,6},{6,7},{7,4},{8,9},{9,10},{10,1... | collective-permute-start | bytes 1572872 | tf_op jit(solution)/shard_map/ppermute | solution.py:21
  397.5 137.0 %collective-permute-start.3 = (bf16[2,32,4096]{2,1,0:T(8,128)(2,1)}, bf16[2,32,4096]{2,1,0:T(8,128)(2,1)}, u32[]{:S(2)}, u32[]{:S(2)}) collective-permute-start(bf16[2,32,4096]{2,1,0:T(8,128)(2,1)} %convert_element_type.79), channel_id=1, source_target_pairs={{0,1},{1,2},{2,3},{3,0},{4,5},{5,6},{6,7},{7,4},{8,9},{9,10},{10,1... | collective-permute-start | bytes 1572872 | tf_op jit(solution)/shard_map/ppermute | solution.py:21
  398.8 12.9 %copy-start.2 = (bf16[2,256,4096]{2,1,0:T(8,128)(2,1)S(1)}, bf16[2,256,4096]{2,1,0:T(8,128)(2,1)}, u32[]{:S(2)}) copy-start(bf16[2,256,4096]{2,1,0:T(8,128)(2,1)} %param.11) | copy-start | bytes 12582916
  408.4 3.2 copy-start
  411.6 42.8 %copy-start.6 = (bf16[2,256,1024]{2,1,0:T(8,128)(2,1)S(1)}, bf16[2,256,1024]{2,1,0:T(8,128)(2,1)}, u32[]{:S(2)}) copy-start(bf16[2,256,1024]{2,1,0:T(8,128)(2,1)} %param.12) | copy-start | bytes 3145732
  461.8 18.6 %all-to-all-start.2 = ((bf16[4,256,256]{1,2,0:T(8,128)(2,1)}), bf16[4,256,256]{1,2,0:T(8,128)(2,1)S(1)}, u32[]{:S(2)}, u32[]{:S(2)}) async-start(bf16[4,256,256]{1,2,0:T(8,128)(2,1)} %bitcast.12), calls=%async_computation.2 | async-start | bytes 1048576 | tf_op jit(solution)/shard_map/all_to_all | solution.py:31
  465.9 7.2 %copy-start.7 = (bf16[2,256,1024]{2,1,0:T(8,128)(2,1)S(1)}, bf16[2,256,1024]{2,1,0:T(8,128)(2,1)}, u32[]{:S(2)}) copy-start(bf16[2,256,1024]{2,1,0:T(8,128)(2,1)} %param.12) | copy-start | bytes 3145732
  480.4 31.7 %all-to-all-start.1 = ((bf16[4,256,256]{1,2,0:T(8,128)(2,1)}), bf16[4,256,256]{1,2,0:T(8,128)(2,1)S(1)}, u32[]{:S(2)}, u32[]{:S(2)}) async-start(bf16[4,256,256]{1,2,0:T(8,128)(2,1)} %bitcast.6), calls=%async_computation.1 | async-start | bytes 1048576 | tf_op jit(solution)/shard_map/all_to_all | solution.py:31
  490.7 43.9 %copy-start.3 = (bf16[1,2,32,4096]{3,2,1,0:T(8,128)(2,1)S(1)}, bf16[1,2,32,4096]{3,2,1,0:T(8,128)(2,1)}, u32[]{:S(2)}) copy-start(bf16[1,2,32,4096]{3,2,1,0:T(8,128)(2,1)} %reduce-scatter.8.cloned.1.call-done) | copy-start | bytes 1572868
Sparse Core Ops, SparseCore 0:
  34.1 353.7 reduce-scatter.3
  390.4 64.0 reduce-scatter.5
  456.8 29.4 reduce-scatter.7
